TPU v7x, 32 devices: a whole 2x2x4 slice. The times are simulated.
32 devices in a mesh: pa: 4 (over y, core), pb: 8 (over z, x).
Axes of the slice: x: 2, y: 2, z: 4, core: 2. Of those that a mesh axis runs over, the one named last changes fastest.
Arguments:
- excitons: bfloat16 [2, 512, 1024], P(None, 'pa', 'pb'), may hold values from -6 to 6
- screened: bfloat16 [16384, 16384], P('pa', 'pb'), may hold values from -0.25 to 0.25
- phi_val: bfloat16 [16384, 512], P('pa'), may hold values from -0.25 to 0.25
- phi_con: bfloat16 [16384, 1024], P('pb'), may hold values from -0.1875 to 0.1875
Outputs:
- kernel_out: bfloat16 [2, 512, 1024], P(None, 'pa', 'pb')
All inputs are finite; a program needn't handle non-finite values.
Results may differ from a plain program's by a relative error of at most 0.0057.
Values may be sent and summed in bfloat16 or wider, within the bound.
No kernel may reach another device: no remote copies, remote signals or barrier semaphores. Data moves between devices by JAX's collectives and lax.ppermute only.
A program may use at most 192 MiB of HBM per device.

v0:
```python
import jax
import jax.numpy as jnp
from jax import lax
from jax.sharding import PartitionSpec as P


def local(excitons, screened, phi_val, phi_con):
    high = lax.Precision.HIGHEST
    val_rows = lax.all_gather(excitons, "pb", axis=2, tiled=True)
    half_exp = jnp.einsum(
        "evc,qc->evq",
        lax.all_gather(val_rows, "pa", axis=1, tiled=True),
        phi_con,
        preferred_element_type=jnp.float32,
    ).astype(jnp.bfloat16)
    expanded = jnp.einsum("pv,evq->epq", phi_val, half_exp, preferred_element_type=jnp.float32)
    weighted = (screened.astype(jnp.float32)[None] * expanded).astype(jnp.bfloat16)
    partial_value = jnp.einsum("pv,epq->evq", phi_val, weighted, preferred_element_type=jnp.float32)
    con_float = phi_con.astype(jnp.float32)
    terms = jnp.einsum("evq,qc->evc", partial_value, con_float, precision=high)
    columns = lax.psum_scatter(terms, "pb", scatter_dimension=2, tiled=True)
    result = lax.psum_scatter(columns, "pa", scatter_dimension=1, tiled=True)
    return result.astype(jnp.bfloat16)


def solution(mesh):
    placed = (P(None, "pa", "pb"), P("pa", "pb"), P("pa", None), P("pb", None))
    return jax.shard_map(
        local, mesh=mesh, in_specs=placed, out_specs=P(None, "pa", "pb"), check_vma=False
    )
```

profile of v0, /device:TPU:0, one launch (start us, length us, event | category | flops | bytes accessed | tf_op | source)
XLA Modules:
  0.0 260.3 jit_solution(2940196024953835160)
XLA Ops:
  6.5 0.0 all-gather.2.cloned.1.call-start
  6.5 31.1 %all_gather.6 = bf16[2,128,1024]{2,1,0:T(8,128)(2,1)} all-gather(bf16[2,128,128]{2,1,0:T(8,128)(2,1)} %param.4), channel_id=1, replica_groups=mesh['pa'=4,'pb'=8] {'pb'}, dimensions={2}, use_global_device_ids=true | all-gather | bytes 589824 | tf_op jit(solution)/shard_map/all_gather | solution.py:9
  37.6 0.0 all-gather.2.cloned.1.call-update
  37.6 0.0 reduce-scatter.3.cloned.1.call-start
  37.7 18.8 %convert_element_type.13 = f32[4096,2048]{1,0:T(8,128)} convert(bf16[4096,2048]{1,0:T(8,128)(2,1)} %param.5) | non-fusion elementwise | flops 8388608 | bytes 50331648 | tf_op jit(solution)/shard_map/convert_element_type | solution.py:17
  56.5 2.3 all-gather.2.cloned.1.call-done
  58.8 9.3 %fusion.11 = bf16[2,512,2048]{2,1,0:T(8,128)(2,1)} fusion(bf16[2,512,1024]{2,1,0:T(8,128)(2,1)} %all-gather.2.cloned.1.call-done, bf16[2048,1024]{1,0:T(8,128)(2,1)} %param.7), kind=kOutput, calls=%fused_computation.9 | convolution fusion | flops 4294967296 | bytes 10485760 | tf_op jit(solution)/shard_map/evc,qc->evq/dot_general | solution.py:10
  68.1 33.7 %fusion.26 = bf16[2,4096,2048]{2,1,0:T(8,128)(2,1)} fusion(f32[4096,2048]{1,0:T(8,128)} %convert_element_type.13, bf16[4096,512]{1,0:T(8,128)(2,1)} %param.6, bf16[2,512,2048]{2,1,0:T(8,128)(2,1)} %fusion.11), kind=kOutput, calls=%fused_computation.1.clone.clone.1 | convolution fusion | flops 17213423616 | bytes 75497472 | tf_op jit(solution)/shard_map/pv,evq->epq/dot_general | solution.py:16
  101.8 0.0 copy-start
  101.8 22.9 %fusion.1 = f32[2,2048,512]{1,2,0:T(8,128)S(1)} fusion(bf16[4096,512]{1,0:T(8,128)(2,1)} %param.6, bf16[2,4096,2048]{2,1,0:T(8,128)(2,1)} %fusion.26), kind=kOutput, calls=%fused_computation.2 | convolution fusion | flops 17179869184 | bytes 46137344 | tf_op jit(solution)/shard_map/pv,epq->evq/dot_general | solution.py:18
  124.7 0.0 copy-done
  124.7 14.9 %fusion.4 = f32[2,512,1024]{2,1,0:T(8,128)} fusion(f32[2,2048,512]{1,2,0:T(8,128)S(1)} %fusion.1, bf16[2048,1024]{1,0:T(8,128)(2,1)S(1)} %copy-done), kind=kOutput, calls=%fused_computation.4 | convolution fusion | flops 25769803776 | bytes 16777216 | tf_op jit(solution)/shard_map/evq,qc->evc/dot_general | solution.py:20
  139.6 0.0 reduce-scatter.3.cloned.1.call-update
  139.6 0.0 reduce-scatter.5.cloned.1.call-start
  139.6 88.8 %reduce-scatter.3.cloned.1.call-done = f32[2,512,128]{2,1,0:T(8,128)} async-done(((f32[2,512,1024]{2,1,0:T(8,128)}), f32[2,512,128]{2,1,0:T(8,128)}) %reduce-scatter.3.cloned.1.call-update) | async-done | bytes 524304 | tf_op jit(solution)/shard_map/reduce_scatter | solution.py:21
  228.4 0.0 reduce-scatter.5.cloned.1.call-update
  228.4 23.8 %reduce-scatter.5.cloned.1.call-done = f32[2,128,128]{2,1,0:T(8,128)} async-done(((f32[2,512,128]{2,1,0:T(8,128)}), f32[2,128,128]{2,1,0:T(8,128)}) %reduce-scatter.5.cloned.1.call-update) | async-done | bytes 131088 | tf_op jit(solution)/shard_map/reduce_scatter | solution.py:22
  252.3 1.5 convert_element_type.16
Async XLA Ops:
  6.5 52.3 %all-gather.2.cloned.1.call-start = ((), (), s32[]{:S(2)}) async-start(), calls=%async_computation.2 | async-start | bytes 2621440 | tf_op jit(solution)/shard_map/all_gather | solution.py:12
  37.6 190.8 %reduce-scatter.3.cloned.1.call-start = ((), (), s32[]{:S(2)}) async-start(), calls=%async_computation.3 | async-start | bytes 4718592 | tf_op jit(solution)/shard_map/reduce_scatter | solution.py:21
  101.8 22.9 %copy-start = (bf16[2048,1024]{1,0:T(8,128)(2,1)S(1)}, bf16[2048,1024]{1,0:T(8,128)(2,1)}, u32[]{:S(2)}) copy-start(bf16[2048,1024]{1,0:T(8,128)(2,1)} %param.7) | copy-start | bytes 12582916
  139.6 112.7 %reduce-scatter.5.cloned.1.call-start = ((), (), s32[]{:S(2)}) async-start(), calls=%async_computation.4 | async-start | bytes 655360 | tf_op jit(solution)/shard_map/reduce_scatter | solution.py:22
Sparse Core Ops, SparseCore 0:
  37.8 20.9 all-gather.1
  139.7 88.6 reduce-scatter.2
  230.9 21.3 reduce-scatter.4
where the time goes:
time: 261 us; the launch traced here: 260 us
  waiting for transfers between devices  115 us (44%)
  matrix products  80.8 us (31%)
  blocking collectives  31.1 us (12%)
  other arithmetic  20.4 us (8%)
  between operations  13.1 us (5%)
    reduce_scatter x1, waiting for transfers between devices, local(): columns = lax.psum_scatter(terms, 'pb', scatter_dimension=2, tiled=True)  88.8 us
    dot_general x1, matrix products, local(): jnp.einsum('pv,evq->epq', phi_val, half_exp, preferred_element_type=jnp.f...  33.7 us
    all_gather x1, blocking collectives, local(): val_rows = lax.all_gather(excitons, 'pb', axis=2, tiled=True)  31.1 us
    reduce_scatter x1, waiting for transfers between devices, local(): result = lax.psum_scatter(columns, 'pa', scatter_dimension=1, tiled=True)  23.8 us
    dot_general x1, matrix products, local(): jnp.einsum('pv,epq->evq', phi_val, weighted, preferred_element_type=jnp.f...  22.9 us
    convert_element_type x1, other arithmetic, local(): screened.astype(jnp.float32)[None] * expanded  18.8 us
    dot_general x1, matrix products, local(): terms = jnp.einsum('evq,qc->evc', partial_value, con_float, precision=high)  14.9 us
    dot_general x1, matrix products, local(): jnp.einsum('evc,qc->evq', lax.all_gather(val_rows, 'pa', axis=1, tiled=Tr...  9.34 us
  transfers between devices with their start and end apart: 3, of which 3 were waited for; matrix products, arithmetic and copies ran while one was open for 7% of the time, Pallas kernels for 0%

commit v1 on v0

--- a/solution.py
+++ b/solution.py
@@ -5,13 +5,42 @@
 
 
 def local(excitons, screened, phi_val, phi_con):
+
+    def refer_the_lane(xx, lane_axis, frame_in):
+        raw_out, current_arr, block_out = (
+            lax.axis_size(lane_axis),
+            lax.axis_index(lane_axis),
+            xx.shape[1],
+        )
+        known, v_next = ([], [])
+        item_now = tmp = xx
+        for q in range(raw_out // 2 + 1):
+            known.append(frame_in(item_now, (current_arr - q) % raw_out * block_out))
+            if 0 < q < raw_out - raw_out // 2:
+                v_next.append(frame_in(tmp, (current_arr + q) % raw_out * block_out))
+            grid = []
+            for j0 in range(raw_out):
+                grid.append((j0, (j0 + 1) % raw_out))
+            item_now = lax.ppermute(item_now, lane_axis, grid)
+            rack = []
+            for j0 in range(raw_out):
+                rack.append((j0, (j0 - 1) % raw_out))
+            tmp = lax.ppermute(tmp, lane_axis, rack)
+        piece_now = jnp.roll(
+            jnp.concatenate([*known[::-1], *v_next], axis=1),
+            shift=(current_arr - raw_out // 2) * known[0].shape[1],
+            axis=1,
+        )
+        return piece_now
+
     high = lax.Precision.HIGHEST
     val_rows = lax.all_gather(excitons, "pb", axis=2, tiled=True)
-    half_exp = jnp.einsum(
-        "evc,qc->evq",
-        lax.all_gather(val_rows, "pa", axis=1, tiled=True),
-        phi_con,
-        preferred_element_type=jnp.float32,
+    half_exp = refer_the_lane(
+        val_rows,
+        "pa",
+        lambda part, start: jnp.einsum(
+            "evc,qc->evq", part, phi_con, preferred_element_type=jnp.float32
+        ),
     ).astype(jnp.bfloat16)
     expanded = jnp.einsum("pv,evq->epq", phi_val, half_exp, preferred_element_type=jnp.float32)
     weighted = (screened.astype(jnp.float32)[None] * expanded).astype(jnp.bfloat16)

time: 261 us -> 274 us (1.050)
  waiting for transfers between devices: 115 us -> 120 us
  local copies, waits for them, and re-layouts: 0.01 us -> 4.18 us
  matrix products: 80.8 us -> 84.7 us
    ppermute x0 -> x3, waiting for transfers between devices: none -> 8.61 us  [the longest x2 8.61 us: refer_the_lane(): item_now = lax.ppermute(item_now, lane_axis, grid)]
    dot_general x1 -> x4, matrix products: 9.34 us -> 13.5 us  [local(): jnp.einsum('evc,qc->evq', part, phi_con, preferred_element_type=jnp.float32)]
    unnamed x2 -> x7, local copies, waits for them, and re-layouts: 0.01 us -> 3.1 us
  transfers between devices with their start and end apart: 3 -> 5, of which waited for: 3 -> 3; matrix products, arithmetic and copies ran while one was open for 7% -> 11% of each run, Pallas kernels for 0% -> 0%
where the time goes in v1:
time: 274 us
  waiting for transfers between devices  120 us (44%)
  matrix products  84.7 us (31%)
  blocking collectives  29.8 us (11%)
  other arithmetic  20.2 us (7%)
  between operations  13.4 us (5%)
  local copies, waits for them, and re-layouts  4.18 us (2%)
    reduce_scatter x1, waiting for transfers between devices, local(): columns = lax.psum_scatter(terms, 'pb', scatter_dimension=2, tiled=True)  87.6 us
    dot_general x1, matrix products, local(): jnp.einsum('pv,evq->epq', phi_val, half_exp, preferred_element_type=jnp.f...  33.6 us
    all_gather x1, blocking collectives, local(): val_rows = lax.all_gather(excitons, 'pb', axis=2, tiled=True)  29.8 us
    reduce_scatter x1, waiting for transfers between devices, local(): result = lax.psum_scatter(columns, 'pa', scatter_dimension=1, tiled=True)  23.8 us
    dot_general x1, matrix products, local(): jnp.einsum('pv,epq->evq', phi_val, weighted, preferred_element_type=jnp.f...  22.9 us
    convert_element_type x1, other arithmetic, local(): screened.astype(jnp.float32)[None] * expanded  18.7 us
    dot_general x1, matrix products, local(): terms = jnp.einsum('evq,qc->evc', partial_value, con_float, precision=high)  14.7 us
    dot_general x4, matrix products, local(): jnp.einsum('evc,qc->evq', part, phi_con, preferred_element_type=jnp.float32)  13.5 us
  transfers between devices with their start and end apart: 5, of which 3 were waited for; matrix products, arithmetic and copies ran while one was open for 11% of the time, Pallas kernels for 0%

profile of v1, /device:TPU:0, one launch (start us, length us, event | category | flops | bytes accessed | tf_op | source)
XLA Modules:
  0.0 274.2 jit_solution(13711400594753581959)
XLA Ops:
  6.5 0.0 reduce-scatter.3.cloned.1.call-start
  6.5 29.8 %all_gather.3 = bf16[2,128,1024]{2,1,0:T(8,128)(2,1)S(1)} all-gather(bf16[2,128,128]{2,1,0:T(8,128)(2,1)} %param.4), channel_id=1, replica_groups=mesh['pa'=4,'pb'=8] {'pb'}, dimensions={2}, use_global_device_ids=true | all-gather | bytes 589824 | tf_op jit(solution)/shard_map/all_gather | solution.py:37
  36.3 0.0 collective-permute-start
  36.3 8.6 %collective-permute-done = bf16[2,128,1024]{2,1,0:T(8,128)(2,1)S(1)} collective-permute-done((bf16[2,128,1024]{2,1,0:T(8,128)(2,1)S(1)}, bf16[2,128,1024]{2,1,0:T(8,128)(2,1)S(1)}, u32[]{:S(2)}, u32[]{:S(2)}) %collective-permute-start) | collective-permute-done | bytes 524320 | tf_op jit(solution)/shard_map/ppermute | solution.py:24
  44.9 0.0 collective-permute-start.1
  44.9 1.7 collective-permute-start.2
  46.7 18.7 %convert_element_type.13 = f32[4096,2048]{1,0:T(8,128)} convert(bf16[4096,2048]{1,0:T(8,128)(2,1)} %param.5) | non-fusion elementwise | flops 8388608 | bytes 50331648 | tf_op jit(solution)/shard_map/convert_element_type | solution.py:46
  65.4 0.0 copy-start
  65.4 0.0 collective-permute-done.1
  65.4 4.6 %constant_dynamic-update-slice_fusion.7 = (bf16[2,1024,2048]{2,1,0:T(8,128)(2,1)}, bf16[2,128,2048]{2,1,0:T(8,128)(2,1)S(1)}) fusion(bf16[2,128,1024]{2,1,0:T(8,128)(2,1)S(1)} %collective-permute-done.1, bf16[2048,1024]{1,0:T(8,128)(2,1)} %param.7), kind=kOutput, calls=%fused_computation.25 | convolution fusion | flops 1073741824 | bytes 6815744 | tf_op jit(solution)/shard_map/evc,qc->evq/dot_general | solution.py:41
  69.9 4.4 %constant_dynamic-update-slice_fusion.6 = (bf16[2,1024,2048]{2,1,0:T(8,128)(2,1)}, bf16[2,128,2048]{2,1,0:T(8,128)(2,1)S(1)}) fusion(bf16[2,1024,2048]{2,1,0:T(8,128)(2,1)} %get-tuple-element.5, bf16[2,128,1024]{2,1,0:T(8,128)(2,1)S(1)} %collective-permute-done, bf16[2048,1024]{1,0:T(8,128)(2,1)} %param.7), kind=kOutput, calls=%fused_computation.24 | convolution fusion | flops 1073741824 | bytes 6815744 | tf_op jit(solution)/shard_map/evc,qc->evq/dot_general | solution.py:41
  74.4 0.0 copy-done
  74.4 2.3 constant_dynamic-update-slice_fusion.5
  76.6 0.0 collective-permute-done.2
  76.6 2.2 constant_dynamic-update-slice_fusion.4
  78.9 1.0 constant_dynamic-update-slice_fusion.3
  79.9 1.0 constant_dynamic-update-slice_fusion.2
  80.9 1.0 constant_dynamic-update-slice_fusion.1
  82.0 1.1 constant_dynamic-update-slice_fusion
  83.0 33.6 %fusion.31 = bf16[2,4096,2048]{2,1,0:T(8,128)(2,1)} fusion(f32[4096,2048]{1,0:T(8,128)} %convert_element_type.13, bf16[2,1024,2048]{2,1,0:T(8,128)(2,1)} %constant_dynamic-update-slice_fusion, s32[]{:T(128)S(6)} %select_n.14, bf16[4096,512]{1,0:T(8,128)(2,1)} %param.6), kind=kOutput, calls=%fused_computation.1.clone.clone.1 | convolution fusion | flops 17213423616 | bytes 75497472 | tf_op jit(solution)/shard_map/pv,evq->epq/dot_general | solution.py:45
  116.7 0.0 copy-start.1
  116.7 22.9 %fusion.1 = f32[2,2048,512]{1,2,0:T(8,128)S(1)} fusion(bf16[4096,512]{1,0:T(8,128)(2,1)} %param.6, bf16[2,4096,2048]{2,1,0:T(8,128)(2,1)} %fusion.31), kind=kOutput, calls=%fused_computation.2 | convolution fusion | flops 17179869184 | bytes 46137344 | tf_op jit(solution)/shard_map/pv,epq->evq/dot_general | solution.py:47
  139.5 0.0 copy-done.1
  139.5 14.7 %fusion.4 = f32[2,512,1024]{2,1,0:T(8,128)} fusion(f32[2,2048,512]{1,2,0:T(8,128)S(1)} %fusion.1, bf16[2048,1024]{1,0:T(8,128)(2,1)S(1)} %copy-done.1), kind=kOutput, calls=%fused_computation.4 | convolution fusion | flops 25769803776 | bytes 16777216 | tf_op jit(solution)/shard_map/evq,qc->evc/dot_general | solution.py:49
  154.3 0.0 reduce-scatter.3.cloned.1.call-update
  154.3 0.0 reduce-scatter.5.cloned.1.call-start
  154.4 87.6 %reduce-scatter.3.cloned.1.call-done = f32[2,512,128]{2,1,0:T(8,128)} async-done(((f32[2,512,1024]{2,1,0:T(8,128)}), f32[2,512,128]{2,1,0:T(8,128)}) %reduce-scatter.3.cloned.1.call-update) | async-done | bytes 524304 | tf_op jit(solution)/shard_map/reduce_scatter | solution.py:50
  242.0 0.0 reduce-scatter.5.cloned.1.call-update
  242.0 23.8 %reduce-scatter.5.cloned.1.call-done = f32[2,128,128]{2,1,0:T(8,128)} async-done(((f32[2,512,128]{2,1,0:T(8,128)}), f32[2,128,128]{2,1,0:T(8,128)}) %reduce-scatter.5.cloned.1.call-update) | async-done | bytes 131088 | tf_op jit(solution)/shard_map/reduce_scatter | solution.py:51
  265.8 1.5 convert_element_type.16
Async XLA Ops:
  6.5 235.4 %reduce-scatter.3.cloned.1.call-start = ((), (), s32[]{:S(2)}) async-start(), calls=%async_computation.2 | async-start | bytes 4718592 | tf_op jit(solution)/shard_map/reduce_scatter | solution.py:50
  36.3 8.6 %collective-permute-start = (bf16[2,128,1024]{2,1,0:T(8,128)(2,1)S(1)}, bf16[2,128,1024]{2,1,0:T(8,128)(2,1)S(1)}, u32[]{:S(2)}, u32[]{:S(2)}) collective-permute-start(bf16[2,128,1024]{2,1,0:T(8,128)(2,1)S(1)} %all_gather.3), channel_id=1, source_target_pairs={{0,8},{8,16},{16,24},{24,0},{1,9},{9,17},{17,25},{25,1},{2,10},{10... | collective-permute-start | bytes 1572872 | tf_op jit(solution)/shard_map/ppermute | solution.py:24
  44.9 20.4 %collective-permute-start.1 = (bf16[2,128,1024]{2,1,0:T(8,128)(2,1)S(1)}, bf16[2,128,1024]{2,1,0:T(8,128)(2,1)S(1)}, u32[]{:S(2)}, u32[]{:S(2)}) collective-permute-start(bf16[2,128,1024]{2,1,0:T(8,128)(2,1)S(1)} %collective-permute-done), channel_id=1, source_target_pairs={{0,8},{8,16},{16,24},{24,0},{1,9},{9,17},{17,25},{25,1},{2,10},{10... | collective-permute-start | bytes 1572872 | tf_op jit(solution)/shard_map/ppermute | solution.py:24
  44.9 31.7 %collective-permute-start.2 = (bf16[2,128,1024]{2,1,0:T(8,128)(2,1)S(1)}, bf16[2,128,1024]{2,1,0:T(8,128)(2,1)S(1)}, u32[]{:S(2)}, u32[]{:S(2)}) collective-permute-start(bf16[2,128,1024]{2,1,0:T(8,128)(2,1)S(1)} %all_gather.3), channel_id=1, source_target_pairs={{0,24},{8,0},{16,8},{24,16},{1,25},{9,1},{17,9},{25,17},{2,26},{10... | collective-permute-start | bytes 1572872 | tf_op jit(solution)/shard_map/ppermute | solution.py:28
  65.4 9.0 %copy-start = (bf16[2048,1024]{1,0:T(8,128)(2,1)S(1)}, bf16[2048,1024]{1,0:T(8,128)(2,1)}, u32[]{:S(2)}) copy-start(bf16[2048,1024]{1,0:T(8,128)(2,1)} %param.7) | copy-start | bytes 12582916
  116.7 22.9 %copy-start.1 = (bf16[2048,1024]{1,0:T(8,128)(2,1)S(1)}, bf16[2048,1024]{1,0:T(8,128)(2,1)}, u32[]{:S(2)}) copy-start(bf16[2048,1024]{1,0:T(8,128)(2,1)} %param.7) | copy-start | bytes 12582916
  154.3 111.5 %reduce-scatter.5.cloned.1.call-start = ((), (), s32[]{:S(2)}) async-start(), calls=%async_computation.3 | async-start | bytes 655360 | tf_op jit(solution)/shard_map/reduce_scatter | solution.py:51
Sparse Core Ops, SparseCore 0:
  154.4 87.4 reduce-scatter.2
  244.4 21.2 reduce-scatter.4
